TPU v7x, 32 devices: a whole 2x2x4 slice. The times are simulated.
32 devices in a mesh: cls: 8 (over z, x), rot: 4 (over y, core).
Axes of the slice: x: 2, y: 2, z: 4, core: 2. Of those that a mesh axis runs over, the one named last changes fastest.
Arguments:
- particles: bfloat16 [384, 64, 384], P('cls'), may hold values from -6 to 6
- references: bfloat16 [512, 64, 384], P('cls'), may hold values from -0.09 to 0.09
- noise_weights: float32 [64], replicated, may hold values from 0.1 to 1
- offsets: int32 [384], P('cls'), may hold values from 0 to 383
- sig_classes: int32 [384, 3], P('cls'), may hold values from 0 to 511, as said below
Outputs:
- log_evidence: float32 [384], P('cls')
- class_sums: float32 [512, 64, 384], P('cls', 'rot')
Inputs may be any that keep to these rules, and one draw needn't show every extreme that they name: `sig_classes`: each particle lists 3 different classes. In each aligned block of 48 particles (those of one index of cls), at most 36 particles list a class of one owner (one value of id // 64); one owner, the same for all blocks, is listed by exactly 36 particles of every block.
All inputs are finite; a program needn't handle non-finite values.
Results may differ from a plain program's by a relative error of at most 0.0047.
Values may be sent and summed in bfloat16 or wider, within the bound.
A program may use at most 128 MiB of HBM per device.

v0:
```python
import jax
import jax.numpy as jnp
from jax import lax
from jax.sharding import PartitionSpec as P

ROTS = 48


def shift_table(angle_shift, angle_count, sign):
    rows = jnp.arange(angle_count, dtype=jnp.int32)[:, None]
    cols = jnp.arange(angle_count, dtype=jnp.int32)[None, :]
    target = (cols + sign * angle_shift) % angle_count
    return rows == target


def shards(particles, references, noise_weights, offsets, sig_classes):
    owner_count = lax.axis_size("cls")
    split_count = lax.axis_size("rot")
    particle_count, cycle_count, angle_count = particles.shape
    class_local = references.shape[0]
    list_length = sig_classes.shape[1]
    capacity = 2 * list_length * particle_count // owner_count
    angle_step = angle_count // ROTS
    block_size = 6
    rot_local = ROTS // split_count
    rot_first = lax.axis_index("rot") * rot_local
    angle_rows = jnp.arange(angle_count, dtype=jnp.int32)
    source_index = (angle_rows[None, :] + offsets[:, None]) % angle_count
    align_tables = jnp.where(
        angle_rows[None, :, None] == source_index[:, None, :], 1.0, 0.0
    ).astype(jnp.bfloat16)
    aligned = jnp.einsum(
        "pra,pab->prb", particles, align_tables, preferred_element_type=jnp.float32
    ).astype(jnp.bfloat16)
    class_iota = jnp.arange(owner_count * class_local, dtype=jnp.int32)
    listed = jnp.sum(
        (sig_classes[:, :, None] == class_iota[None, None, :]).astype(jnp.float32), axis=1
    )
    listed = listed.reshape(particle_count, owner_count, class_local)
    paired = jnp.max(listed, axis=2).astype(jnp.int32)
    slot_index = jnp.cumsum(paired, axis=0) - paired
    slot_iota = jnp.arange(capacity, dtype=jnp.int32)
    hit_slot = (slot_index.T[:, None, :] == slot_iota[None, :, None]) & (paired.T[:, None, :] > 0)
    select = jnp.where(hit_slot, 1.0, 0.0).astype(jnp.float32)
    select_half = select.astype(jnp.bfloat16)
    outbound = jnp.einsum(
        "osp,pra->osra", select_half, aligned, preferred_element_type=jnp.float32
    ).astype(jnp.bfloat16)
    out_mask = jnp.einsum(
        "osp,poc->osc", select_half, listed.astype(jnp.bfloat16), preferred_element_type=jnp.float32
    ).astype(jnp.bfloat16)
    inbound, in_mask = (
        lax.all_to_all(outbound, "cls", split_axis=0, concat_axis=0, tiled=True),
        lax.all_to_all(out_mask, "cls", split_axis=0, concat_axis=0, tiled=True),
    )
    slot_total = owner_count * capacity
    inbound_flat = inbound.reshape(slot_total, cycle_count * angle_count)
    mask_flat = in_mask.reshape(slot_total, class_local).astype(jnp.float32)
    own_images = references.astype(jnp.float32)
    own_weights = noise_weights[None, :, None]
    weighted = (own_images * own_weights).astype(jnp.bfloat16)
    weighted_rows = weighted.reshape(class_local * cycle_count, angle_count)
    energy = 0.5 * jnp.sum(own_weights * own_images * own_images, axis=(1, 2))
    turn_count = rot_local // block_size

    def score_block(turn_index, collected):
        rot_start = turn_index * block_size
        for member in range(block_size):
            angle_shift = (rot_first + rot_start + member) * angle_step
            table = jnp.where(shift_table(angle_shift, angle_count, -1), 1.0, 0.0).astype(
                jnp.bfloat16
            )
            rotated = jnp.dot(weighted_rows, table, preferred_element_type=jnp.float32).astype(
                jnp.bfloat16
            )
            rotated = rotated.reshape(class_local, cycle_count * angle_count)
            block_scores = jnp.einsum(
                "sx,cx->sc", inbound_flat, rotated, preferred_element_type=jnp.float32
            )
            collected = lax.dynamic_update_index_in_dim(
                collected, block_scores, rot_start + member, 0
            )
        return collected

    start_scores = jnp.zeros((rot_local, slot_total, class_local), jnp.float32)
    scores = lax.fori_loop(0, turn_count, score_block, start_scores)
    scores = jnp.transpose(scores, (1, 0, 2)) - energy[None, None, :]
    exponentials = jnp.exp(scores) * mask_flat.reshape(slot_total, 1, class_local)
    slot_sums = jnp.sum(exponentials, axis=(1, 2))
    returned = lax.all_to_all(
        slot_sums.reshape(owner_count, capacity), "cls", split_axis=0, concat_axis=0, tiled=True
    )
    evidence = jnp.einsum("os,osp->p", returned, select, precision=lax.Precision.HIGHEST)
    evidence = lax.psum(evidence, "rot")
    log_evidence = jnp.log(evidence)
    inverse = 1.0 / evidence
    slot_inverse = jnp.einsum("osp,p->os", select, inverse, precision=lax.Precision.HIGHEST)
    inverse_in = lax.all_to_all(slot_inverse, "cls", split_axis=0, concat_axis=0, tiled=True)
    posterior = (exponentials * inverse_in.reshape(slot_total, 1, 1)).astype(jnp.bfloat16)

    def add_block(turn_index, running):
        rot_start = turn_index * block_size
        for member in range(block_size):
            angle_shift = (rot_first + rot_start + member) * angle_step
            weight_column = lax.dynamic_index_in_dim(
                posterior, rot_start + member, axis=1, keepdims=False
            )
            product = jnp.einsum(
                "sc,sx->cx", weight_column, inbound_flat, preferred_element_type=jnp.float32
            )
            product = product.reshape(class_local * cycle_count, angle_count)
            table = jnp.where(shift_table(angle_shift, angle_count, 1), 1.0, 0.0).astype(
                jnp.float32
            )
            running = running + jnp.dot(product, table, precision=lax.Precision.HIGHEST)
        return running

    start_sums = jnp.zeros((class_local * cycle_count, angle_count), jnp.float32)
    class_part = lax.fori_loop(0, turn_count, add_block, start_sums)
    class_part = class_part.reshape(class_local, cycle_count, angle_count)
    class_part = lax.psum_scatter(class_part, "rot", scatter_dimension=1, tiled=True)
    return (log_evidence, class_part)


def solution(mesh):
    in_specs = (P("cls", None, None), P("cls", None, None), P(), P("cls"), P("cls", None))
    out_specs = (P("cls"), P("cls", "rot", None))
    return jax.shard_map(shards, mesh=mesh, in_specs=in_specs, out_specs=out_specs, check_vma=False)
```

profile of v0, /device:TPU:0, one launch (start us, length us, event | category | flops | bytes accessed | tf_op | source)
XLA Modules:
  0.0 1176.0 jit_solution(4064791939510101550)
XLA Ops:
  45.1 299.4 %all-to-all-done = bf16[8,36,64,384]{3,2,1,0:T(8,128)(2,1)} async-done(((bf16[8,36,64,384]{3,2,1,0:T(8,128)(2,1)}), bf16[8,36,64,384]{3,2,1,0:T(8,128)(2,1)}, u32[]{:S(2)}, u32[]{:S(2)}) %all-to-all-start) | async-done | bytes 14155808 | tf_op jit(solution)/shard_map/all_to_all | solution.py:53
  344.5 11.8 copy.51
  356.4 302.4 %while.32 = (s32[]{:T(128)}, f32[12,288,64]{1,2,0:T(8,128)S(1)}, s32[]{:T(128)}, bf16[4096,384]{1,0:T(8,128)(2,1)}, bf16[288,24576]{1,0:T(8,128)(2,1)}, /*index=...) while((s32[]{:T(128)}, f32[12,288,64]{1,2,0:T(8,128)S(1)}, ...), condition=%wide.region_4.5_spmd, body=%wide.region_3.4_spmd.sunk | while | flops 12695683072 | bytes 280578880 | solution.py:86
  420.6 10.8 fusion.315
  474.3 10.8 fusion.317
  562.0 10.8 fusion.315
  615.8 10.8 fusion.317
  687.5 425.0 %while.33 = (s32[]{:T(128)}, f32[4096,384]{1,0:T(8,128)}, bf16[288,12,64]{0,2,1:T(8,128)(2,1)S(1)}, bf16[288,24576]{1,0:T(8,128)(2,1)}, s32[]{:T(128)}, /*index=...) while((s32[]{:T(128)}, f32[4096,384]{1,0:T(8,128)}, ...), condition=%wide.region_9.10_spmd.clone, body=%wide.region_8.9_spmd.clone.sunk | while | flops 48935157760 | bytes 311741120 | solution.py:119
  697.1 10.8 fusion.358
  714.1 16.6 %fusion.359 = f32[4096,384]{1,0:T(8,128)} fusion(f32[4096,384]{1,0:T(8,128)} %reshape.445, s32[384]{0:T(512)S(1)} %get-tuple-element.453), kind=kOutput, calls=%fused_computation.116.clone.1 | convolution fusion | flops 7248052224 | bytes 12584448 | tf_op jit(solution)/shard_map/while/body/eval_jaxpr/dot_general | solution.py:115
  730.7 10.8 fusion.356
  747.7 16.8 %fusion.357 = f32[4096,384]{1,0:T(8,128)} fusion(f32[4096,384]{1,0:T(8,128)} %reshape.444, s32[384]{0:T(512)S(1)} %get-tuple-element.452), kind=kOutput, calls=%fused_computation.113.clone.1 | convolution fusion | flops 7248052224 | bytes 12584448 | tf_op jit(solution)/shard_map/while/body/eval_jaxpr/dot_general | solution.py:115
  764.5 10.8 fusion.354
  781.4 16.6 %fusion.355 = f32[4096,384]{1,0:T(8,128)} fusion(f32[4096,384]{1,0:T(8,128)} %reshape.443, s32[384]{0:T(512)S(1)} %get-tuple-element.451), kind=kOutput, calls=%fused_computation.110.clone.1 | convolution fusion | flops 7248052224 | bytes 12584448 | tf_op jit(solution)/shard_map/while/body/eval_jaxpr/dot_general | solution.py:115
  798.0 10.8 fusion.352
  814.9 17.0 %fusion.353 = f32[4096,384]{1,0:T(8,128)} fusion(f32[4096,384]{1,0:T(8,128)} %reshape.442, s32[384]{0:T(512)S(1)} %get-tuple-element.450), kind=kOutput, calls=%fused_computation.107.clone.1 | convolution fusion | flops 7248052224 | bytes 12584448 | tf_op jit(solution)/shard_map/while/body/eval_jaxpr/dot_general | solution.py:115
  831.9 10.8 fusion.350
  848.8 16.7 %fusion.351 = f32[4096,384]{1,0:T(8,128)} fusion(f32[4096,384]{1,0:T(8,128)} %reshape.441, s32[384]{0:T(512)S(1)} %get-tuple-element.449), kind=kOutput, calls=%fused_computation.104.clone.1 | convolution fusion | flops 7248052224 | bytes 12584448 | tf_op jit(solution)/shard_map/while/body/eval_jaxpr/dot_general | solution.py:115
  865.5 10.9 fusion.360
  882.5 21.2 %fusion.361 = f32[4096,384]{1,0:T(8,128)} fusion(f32[4096,384]{1,0:T(8,128)} %fusion.351, f32[4096,384]{1,0:T(8,128)} %fusion.353, f32[4096,384]{1,0:T(8,128)} %fusion.355, f32[4096,384]{1,0:T(8,128)} %fusion.357, f32[4096,384]{1,0:T(8,128)} %fusion.359, f32[4096,384]{1,0:T(8,128)} %get-tuple-element.532, f32[4096,384]{1,0:T(8,128)} %reshape.446, ...), kind=kOutput, calls=%fused_computation.101.clone.1 | convolution fusion | flops 7259062272 | bytes 50333184 | tf_op jit(solution)/shard_map/while/body/eval_jaxpr/dot_general | solution.py:115
  904.0 10.8 fusion.358
  921.0 16.6 %fusion.359 = f32[4096,384]{1,0:T(8,128)} fusion(f32[4096,384]{1,0:T(8,128)} %reshape.445, s32[384]{0:T(512)S(1)} %get-tuple-element.453), kind=kOutput, calls=%fused_computation.116.clone.1 | convolution fusion | flops 7248052224 | bytes 12584448 | tf_op jit(solution)/shard_map/while/body/eval_jaxpr/dot_general | solution.py:115
  937.6 10.8 fusion.356
  954.5 17.0 %fusion.357 = f32[4096,384]{1,0:T(8,128)} fusion(f32[4096,384]{1,0:T(8,128)} %reshape.444, s32[384]{0:T(512)S(1)} %get-tuple-element.452), kind=kOutput, calls=%fused_computation.113.clone.1 | convolution fusion | flops 7248052224 | bytes 12584448 | tf_op jit(solution)/shard_map/while/body/eval_jaxpr/dot_general | solution.py:115
  971.6 10.8 fusion.354
  988.5 16.6 %fusion.355 = f32[4096,384]{1,0:T(8,128)} fusion(f32[4096,384]{1,0:T(8,128)} %reshape.443, s32[384]{0:T(512)S(1)} %get-tuple-element.451), kind=kOutput, calls=%fused_computation.110.clone.1 | convolution fusion | flops 7248052224 | bytes 12584448 | tf_op jit(solution)/shard_map/while/body/eval_jaxpr/dot_general | solution.py:115
  1005.1 10.8 fusion.352
  1022.0 16.7 %fusion.353 = f32[4096,384]{1,0:T(8,128)} fusion(f32[4096,384]{1,0:T(8,128)} %reshape.442, s32[384]{0:T(512)S(1)} %get-tuple-element.450), kind=kOutput, calls=%fused_computation.107.clone.1 | convolution fusion | flops 7248052224 | bytes 12584448 | tf_op jit(solution)/shard_map/while/body/eval_jaxpr/dot_general | solution.py:115
  1055.6 16.8 %fusion.351 = f32[4096,384]{1,0:T(8,128)} fusion(f32[4096,384]{1,0:T(8,128)} %reshape.441, s32[384]{0:T(512)S(1)} %get-tuple-element.449), kind=kOutput, calls=%fused_computation.104.clone.1 | convolution fusion | flops 7248052224 | bytes 12584448 | tf_op jit(solution)/shard_map/while/body/eval_jaxpr/dot_general | solution.py:115
  1072.3 10.9 fusion.360
  1089.3 22.1 %fusion.361 = f32[4096,384]{1,0:T(8,128)} fusion(f32[4096,384]{1,0:T(8,128)} %fusion.351, f32[4096,384]{1,0:T(8,128)} %fusion.353, f32[4096,384]{1,0:T(8,128)} %fusion.355, f32[4096,384]{1,0:T(8,128)} %fusion.357, f32[4096,384]{1,0:T(8,128)} %fusion.359, f32[4096,384]{1,0:T(8,128)} %get-tuple-element.532, f32[4096,384]{1,0:T(8,128)} %reshape.446, ...), kind=kOutput, calls=%fused_computation.101.clone.1 | convolution fusion | flops 7259062272 | bytes 50333184 | tf_op jit(solution)/shard_map/while/body/eval_jaxpr/dot_general | solution.py:115
  1113.8 54.9 %reduce-scatter.2.cloned.1.call-done = f32[64,16,384]{2,1,0:T(8,128)} async-done(((f32[64,64,384]{2,1,0:T(8,128)}), f32[64,16,384]{2,1,0:T(8,128)}) %reduce-scatter.2.cloned.1.call-update) | async-done | bytes 1572880 | tf_op jit(solution)/shard_map/reduce_scatter | solution.py:121
  (151 shorter events, 391.3 us)
Async XLA Ops:
  7.2 10.4 copy-start
  8.5 11.7 copy-start.10
  8.6 11.6 copy-start.8
  9.6 22.6 %all-to-all-start.1 = ((bf16[8,2,1152]{2,1,0:T(2,128)(2,1)}), bf16[8,2,1152]{2,1,0:T(2,128)(2,1)S(1)}, u32[]{:S(2)}, u32[]{:S(2)}) async-start(bf16[8,2,1152]{2,1,0:T(2,128)(2,1)} %reshape.421), calls=%async_computation.1 | async-start | bytes 73728 | tf_op jit(solution)/shard_map/all_to_all | solution.py:54
  32.2 6.2 copy-start.13
  32.2 312.3 %all-to-all-start = ((bf16[8,36,64,384]{3,2,1,0:T(8,128)(2,1)}), bf16[8,36,64,384]{3,2,1,0:T(8,128)(2,1)}, u32[]{:S(2)}, u32[]{:S(2)}) async-start(bf16[8,36,64,384]{3,2,1,0:T(8,128)(2,1)} %copy.45), calls=%async_computation | async-start | bytes 28311552 | tf_op jit(solution)/shard_map/all_to_all | solution.py:53
  356.3 302.5 %copy-start.7 = (f32[288,64]{0,1:T(8,128)S(1)}, f32[288,64]{0,1:T(8,128)}, u32[]{:S(2)}) copy-start(f32[288,64]{0,1:T(8,128)} %copy.47) | copy-start | bytes 221188
  356.4 302.5 %copy-start.12 = (f32[64]{0:T(128)S(1)}, f32[64]{0:T(128)}, u32[]{:S(2)}) copy-start(f32[64]{0:T(128)} %broadcast_multiply_fusion) | copy-start | bytes 772
  356.4 312.8 %copy-start.9 = (s32[8,48]{1,0:T(8,128)S(1)}, s32[8,48]{1,0:T(8,128)}, u32[]{:S(2)}) copy-start(s32[8,48]{1,0:T(8,128)} %copy-done.8) | copy-start | bytes 4612
  356.4 312.8 %copy-start.11 = (pred[8,48]{1,0:T(8,128)(4,1)S(1)}, pred[8,48]{1,0:T(8,128)(4,1)}, u32[]{:S(2)}) copy-start(pred[8,48]{1,0:T(8,128)(4,1)} %copy-done.10) | copy-start | bytes 1156
  420.6 10.8 copy-start.6
  474.3 10.8 copy-start.3
  485.1 8.1 copy-start.5
  493.2 8.1 copy-start.2
  501.3 8.1 copy-start.4
  562.0 10.8 copy-start.6
  615.8 10.8 copy-start.3
  626.6 8.1 copy-start.5
  634.7 8.1 copy-start.2
  642.8 8.1 copy-start.4
  675.1 10.9 copy-start.14
  676.3 9.6 all-to-all-start.3
  679.7 489.0 %reduce-scatter.2.cloned.1.call-start = ((), (), s32[]{:S(2)}) async-start(), calls=%async_computation.5 | async-start | bytes 7864320 | tf_op jit(solution)/shard_map/reduce_scatter | solution.py:121
  1112.6 0.7 copy-start.15
  1112.6 56.1 %copy-start.1 = (bf16[48,64,384]{2,1,0:T(8,128)(2,1)S(1)}, bf16[48,64,384]{2,1,0:T(8,128)(2,1)}, u32[]{:S(2)}) copy-start(bf16[48,64,384]{2,1,0:T(8,128)(2,1)} %param.9) | copy-start | bytes 7077892
Sparse Core Ops, SparseCore 0:
  1112.8 55.8 reduce-scatter.1
where the time goes:
time: 1190 us; the launch traced here: 1180 us
  matrix products  518 us (44%)
  waiting for transfers between devices  361 us (30%)
  local copies, waits for them, and re-layouts  210 us (18%)
  loops' own time  30.9 us (3%)
  starting transfers between devices  16.8 us (1%)
  blocking collectives  15.6 us (1%)
  between operations  14.8 us (1%)
    all_to_all x1, waiting for transfers between devices, shards(): lax.all_to_all(outbound, 'cls', split_axis=0, concat_axis=0, tiled=True)  299 us
    dot_general x12, matrix products, add_block(): running = running + jnp.dot(product, table, precision=lax.Precision.HIGHEST)  211 us
    dot_general x12, matrix products, add_block(): jnp.einsum('sc,sx->cx', weight_column, inbound_flat, preferred_element_ty...  130 us
    dot_general x12, matrix products, score_block(): jnp.einsum('sx,cx->sc', inbound_flat, rotated, preferred_element_type=jnp...  107 us
    reshape x12, local copies, waits for them, and re-layouts, add_block(): product = product.reshape(class_local * cycle_count, angle_count)  73.4 us
    dot_general x12, matrix products, score_block(): jnp.dot(weighted_rows, table, preferred_element_type=jnp.float32)  61.3 us
    reshape x12, local copies, waits for them, and re-layouts, score_block(): rotated = rotated.reshape(class_local, cycle_count * angle_count)  58 us
    convert_element_type x12, local copies, waits for them, and re-layouts, score_block(): jnp.dot(weighted_rows, table, preferred_element_type=jnp.float32)  55.8 us
  transfers between devices with their start and end apart: 4, of which 3 were waited for; matrix products, arithmetic and copies ran while one was open for 2% of the time, Pallas kernels for 0%

commit v1 on v0

v1 whole, which is shorter than its diff:
```python
import functools

import jax
import jax.numpy as jnp
from jax import lax
from jax.experimental import pallas as pl
from jax.experimental.pallas import tpu as pltpu
from jax.sharding import PartitionSpec as P

ROTS = 48
GROUP = 8
LANES = 128
SPAN = LANES // GROUP
BATCH = 8
F32 = jnp.float32
BF16 = jnp.bfloat16


def swap_blocks(pages):
    block = lax.broadcasted_iota(jnp.int32, pages[0].shape, 1) // SPAN
    for step in (1, 2, 4):
        high = (block & step) != 0
        changed = list(pages)
        for low_index in range(GROUP):
            if low_index & step:
                continue
            low_page, high_page = pages[low_index], pages[low_index | step]
            changed[low_index] = jnp.where(high, pltpu.roll(high_page, SPAN * step, 1), low_page)
            changed[low_index | step] = jnp.where(
                high, high_page, pltpu.roll(low_page, LANES - SPAN * step, 1)
            )
        pages = changed
    return pages


def split_angles(rows, flipped):
    flipped[...] = rows.T
    return swap_blocks([flipped[pl.ds(s, ROTS, stride=GROUP), :] for s in range(GROUP)])


def particle_kernel(rot_ref, offset_ref, image_ref, page_ref, rows, flipped):
    first = pl.program_id(0) * GROUP
    cycles, angles = image_ref.shape[1:]
    if cycles < SPAN:
        rows[...] = jnp.zeros_like(rows)
    for member in range(GROUP):
        shift = lax.rem(angles - offset_ref[first + member], angles)
        rows[pl.ds(member * SPAN, cycles), :] = pltpu.roll(
            image_ref[member].astype(F32), shift, 1
        )
    pages = split_angles(rows[...], flipped)
    for member in range(GROUP):
        page_ref[member] = pages[member].astype(BF16)


def reference_kernel(rot_ref, image_ref, weight_ref, page_ref, energy_ref, flipped):
    cycles, angles = image_ref.shape[1:]
    images = image_ref[...].astype(F32)
    weights = weight_ref[...][None]
    weighted = (images * weights).astype(BF16).astype(F32)
    energy = jnp.sum(jnp.sum(weights * images * images, axis=2), axis=1, keepdims=True)
    energy_ref[...] = jnp.broadcast_to(0.5 * energy, energy_ref.shape)
    if cycles < SPAN:
        spare = jnp.zeros((GROUP, SPAN - cycles, angles), F32)
        weighted = jnp.concatenate([weighted, spare], axis=1)
    pages = split_angles(weighted.reshape(LANES, angles), flipped)
    source = lax.broadcasted_iota(jnp.int32, (ROTS, LANES), 0)
    target = lax.broadcasted_iota(jnp.int32, (ROTS, LANES), 1)
    reverse = jnp.where(lax.rem(source + target, ROTS) == 0, 1.0, 0.0).astype(BF16)
    for member in range(GROUP):
        page_ref[member] = lax.dot_general(
            pages[member].astype(BF16), reverse, (((0,), (0,)), ((), ())), preferred_element_type=F32
        ).astype(BF16)


def score_kernel(count_ref, list_ref, image_ref, class_ref, energy_ref, out_ref, held):
    held[...] = jnp.zeros_like(held)
    half = out_ref.shape[0]

    def batch(step, carry):
        products = []
        for member in range(BATCH):
            at = step * BATCH + member
            image = image_ref[list_ref[1, at]]
            products.append(
                jnp.dot(image, class_ref[list_ref[2, at]], preferred_element_type=F32)
            )
        for member in range(BATCH):
            at = step * BATCH + member
            skewed = pltpu.roll(products[member], 0, 1, stride=1, stride_axis=0)
            score = jnp.sum(skewed, axis=0, keepdims=True)
            held[pl.ds(list_ref[0, at], 1), :] = score - energy_ref[pl.ds(list_ref[2, at], 1), :]
        return carry

    lax.fori_loop(0, count_ref[0], batch, 0)
    lane = lax.broadcasted_iota(jnp.int32, (half, LANES), 1)
    low = pltpu.roll(held[pl.ds(0, half), :], LANES - ROTS, 1)
    high = pltpu.roll(held[pl.ds(half, half), :], LANES // 2 - ROTS, 1)
    inside = (lane % (LANES // 2)) < ROTS
    out_ref[...] = jnp.where(inside, jnp.where(lane < LANES // 2, low, high), 0.0)


def sum_kernel(
    count_ref, list_ref, score_ref, image_ref, out_ref, total_ref, weight, sums, flipped
):
    half = score_ref.shape[0]
    particles = total_ref.shape[0]
    class_local, cycles, angles = out_ref.shape
    lane = lax.broadcasted_iota(jnp.int32, (half, LANES), 1)
    inside = (lane % (LANES // 2)) < ROTS
    grown = jnp.where(inside, jnp.exp(score_ref[...]), 0.0)
    lows = jnp.where(lane < LANES // 2, grown, 0.0)
    highs = pltpu.roll(grown - lows, LANES // 2, 1)
    weight[pl.ds(0, half), :] = lows
    weight[pl.ds(half, half), :] = highs
    listed = 2 * half // particles
    total = jnp.zeros((particles, 1), F32)
    for k in range(listed):
        total += jnp.sum(weight[pl.ds(k * particles, particles), :], axis=1, keepdims=True)
    total_ref[...] = jnp.broadcast_to(total, total_ref.shape)
    inverse = 1.0 / total
    for k in range(listed):
        rows = pl.ds(k * particles, particles)
        posterior = weight[rows, :] * inverse
        weight[rows, :] = posterior + pltpu.roll(posterior, LANES - ROTS, 1)
    weight[pl.ds(2 * half, GROUP), :] = jnp.zeros((GROUP, LANES), F32)
    sums[...] = jnp.zeros_like(sums)

    def batch(step, carry):
        products = []
        for member in range(BATCH):
            at = step * BATCH + member
            row = weight[pl.ds(list_ref[0, at], 1), :]
            skewed = pltpu.roll(
                jnp.broadcast_to(row, (ROTS, LANES)), 0, 1, stride=1, stride_axis=0
            )
            image = image_ref[list_ref[1, at]]
            products.append(
                jnp.dot(skewed.astype(BF16)[:, :ROTS], image, preferred_element_type=F32)
            )
        for member in range(BATCH):
            own = list_ref[2, step * BATCH + member]
            sums[own] = sums[own] + products[member]
        return carry

    lax.fori_loop(0, count_ref[0], batch, 0)

    def write(group, carry):
        first = group * GROUP
        pages = swap_blocks([sums[first + member] for member in range(GROUP)])
        for s in range(GROUP):
            flipped[pl.ds(s, ROTS, stride=GROUP), :] = pages[s]
        out_ref[pl.ds(first, GROUP)] = flipped[...].T.reshape(GROUP, SPAN, angles)[:, :cycles]
        return carry

    lax.fori_loop(0, class_local // GROUP, write, 0)


VMEM = pl.BlockSpec(memory_space=pltpu.VMEM)
SMEM = pl.BlockSpec(memory_space=pltpu.SMEM)


def shards(particles, references, noise_weights, offsets, sig_classes):
    owner_count = lax.axis_size("cls")
    split_count = lax.axis_size("rot")
    home_count, cycle_count, angle_count = particles.shape
    class_local = references.shape[0]
    list_length = sig_classes.shape[1]
    particle_count = home_count * owner_count
    cycles = cycle_count // split_count
    pair_count = particle_count * list_length
    half = pair_count // 2
    me = lax.axis_index("cls")
    rot = lax.axis_index("rot").astype(jnp.int32)
    rot_arg = rot.reshape(1)
    limit = pltpu.CompilerParams(vmem_limit_bytes=56 << 20)

    classes = lax.all_gather(sig_classes, "cls", axis=0, tiled=True)
    classes = classes.T.reshape(pair_count)
    pair_iota = jnp.arange(pair_count, dtype=jnp.int32)
    mine = (classes // class_local) == me
    before = pair_iota[None, :] < pair_iota[:, None]
    place = jnp.sum(jnp.where(before & mine[None, :], 1, 0), axis=1)
    count = jnp.sum(mine.astype(jnp.int32))
    slots = jnp.arange(pair_count + BATCH, dtype=jnp.int32)
    hit = (place[None, :] == slots[:, None]) & mine[None, :]
    pick = lambda values: jnp.sum(jnp.where(hit, values[None, :], 0), axis=1)
    unused = jnp.where(slots < count, 0, pair_count)
    work = jnp.stack(
        [
            pick(pair_iota) + unused,
            pick(pair_iota % particle_count),
            pick(classes % class_local),
        ]
    )
    batches = ((count + BATCH - 1) // BATCH).reshape(1)

    image_block = (GROUP, cycles, angle_count)
    pages = pl.pallas_call(
        particle_kernel,
        out_shape=jax.ShapeDtypeStruct((home_count, ROTS, LANES), BF16),
        grid_spec=pltpu.PrefetchScalarGridSpec(
            num_scalar_prefetch=2,
            grid=(home_count // GROUP,),
            in_specs=[pl.BlockSpec(image_block, lambda g, r, o: (g, r[0], 0))],
            out_specs=pl.BlockSpec((GROUP, ROTS, LANES), lambda g, r, o: (g, 0, 0)),
            scratch_shapes=[
                pltpu.VMEM((LANES, angle_count), F32),
                pltpu.VMEM((angle_count, LANES), F32),
            ],
        ),
        name="align_particles",
    )(rot_arg, offsets, particles)
    gathered = lax.all_gather(pages, "cls", axis=0, tiled=True)

    own_weights = lax.dynamic_slice_in_dim(noise_weights, rot * cycles, cycles).reshape(cycles, 1)
    class_pages, energy = pl.pallas_call(
        reference_kernel,
        out_shape=(
            jax.ShapeDtypeStruct((class_local, LANES, LANES), BF16),
            jax.ShapeDtypeStruct((class_local, LANES), F32),
        ),
        grid_spec=pltpu.PrefetchScalarGridSpec(
            num_scalar_prefetch=1,
            grid=(class_local // GROUP,),
            in_specs=[
                pl.BlockSpec(image_block, lambda g, r: (g, r[0], 0)),
                pl.BlockSpec((cycles, 1), lambda g, r: (0, 0)),
            ],
            out_specs=(
                pl.BlockSpec((GROUP, LANES, LANES), lambda g, r: (g, 0, 0)),
                pl.BlockSpec((GROUP, LANES), lambda g, r: (g, 0)),
            ),
            scratch_shapes=[pltpu.VMEM((angle_count, LANES), F32)],
        ),
        name="weight_references",
    )(rot_arg, references, own_weights)

    scores = pl.pallas_call(
        score_kernel,
        out_shape=jax.ShapeDtypeStruct((half, LANES), F32),
        in_specs=[SMEM, SMEM, VMEM, VMEM, VMEM],
        out_specs=VMEM,
        scratch_shapes=[pltpu.VMEM((pair_count + GROUP, LANES), F32)],
        compiler_params=limit,
        name="score_pairs",
    )(batches, work, gathered, class_pages, energy)
    scores = lax.psum(scores, ("cls", "rot"))

    class_sums, total = pl.pallas_call(
        sum_kernel,
        out_shape=(
            jax.ShapeDtypeStruct((class_local, cycles, angle_count), F32),
            jax.ShapeDtypeStruct((particle_count, LANES), F32),
        ),
        in_specs=[SMEM, SMEM, VMEM, VMEM],
        out_specs=(VMEM, VMEM),
        scratch_shapes=[
            pltpu.VMEM((pair_count + GROUP, LANES), F32),
            pltpu.VMEM((class_local, ROTS, LANES), F32),
            pltpu.VMEM((angle_count, LANES), F32),
        ],
        compiler_params=limit,
        name="sum_classes",
    )(batches, work, scores, gathered)
    own_total = lax.dynamic_slice_in_dim(total, me * home_count, home_count)[:, 0]
    return (jnp.log(own_total), class_sums)


def solution(mesh):
    in_specs = (P("cls", None, None), P("cls", None, None), P(), P("cls"), P("cls", None))
    out_specs = (P("cls"), P("cls", "rot", None))
    return jax.shard_map(shards, mesh=mesh, in_specs=in_specs, out_specs=out_specs, check_vma=False)
```

time: 1190 us -> 260 us (0.22); the launches traced: 1180 us -> 259 us
  matrix products: 518 us -> 0 us
  local copies, waits for them, and re-layouts: 210 us -> 2.23 us
  waiting for transfers between devices: 361 us -> 163 us
  Pallas kernels: 0 us -> 45.7 us
  loops' own time: 30.9 us -> 0 us
  starting transfers between devices: 16.8 us -> 0.08 us
  blocking collectives: 15.6 us -> 28.2 us
    dot_general x53 -> x0, matrix products: 518 us -> none  [the longest x12 211 us: add_block(): running = running + jnp.dot(product, table, precision=lax.Precision.HIGHEST)]
    all_to_all x3 -> x0, waiting for transfers between devices: 306 us -> none  [the longest x1 299 us: shards(): lax.all_to_all(outbound, 'cls', split_axis=0, concat_axis=0, tiled=True)]
    reshape x25 -> x3, local copies, waits for them, and re-layouts: 131 us -> 0.76 us  [the longest x2 0.75 us: shards(): lax.dynamic_slice_in_dim(noise_weights, rot * cycles, cycles)]
    psum x0 -> x1, waiting for transfers between devices: none -> 123 us  [shards(): scores = lax.psum(scores, ('cls', 'rot'))]
    convert_element_type x15 -> x0, local copies, waits for them, and re-layouts: 63.9 us -> none  [the longest x12 55.8 us: score_block(): jnp.dot(weighted_rows, table, preferred_element_type=jnp.float32)]
    reduce_scatter x1 -> x0, waiting for transfers between devices: 54.9 us -> none  [shards(): lax.psum_scatter(class_part, 'rot', scatter_dimension=1, tiled=True)]
    pallas_call x0 -> x4, Pallas kernels: none -> 45.7 us  [the longest x1 17 us: shards(): pl.pallas_call(sum_kernel, out_shape=(jax.ShapeDtypeStruct((class_local,...]
    all_gather x0 -> x1, waiting for transfers between devices: none -> 39.8 us  [shards(): gathered = lax.all_gather(pages, 'cls', axis=0, tiled=True)]
  transfers between devices with their start and end apart: 4 -> 2, of which waited for: 3 -> 2; matrix products, arithmetic and copies ran while one was open for 2% -> 2% of each run, Pallas kernels for 0% -> 3%
where the time goes in v1:
time: 260 us; the launch traced here: 259 us
  waiting for transfers between devices  163 us (63%)
  Pallas kernels  45.7 us (18%)
  blocking collectives  28.2 us (11%)
  between operations  14.8 us (6%)
  other arithmetic  5.16 us (2%)
    psum x1, waiting for transfers between devices, shards(): scores = lax.psum(scores, ('cls', 'rot'))  123 us
    all_gather x1, waiting for transfers between devices, shards(): gathered = lax.all_gather(pages, 'cls', axis=0, tiled=True)  39.8 us
    all_gather x1, blocking collectives, shards(): classes = lax.all_gather(sig_classes, 'cls', axis=0, tiled=True)  28.2 us
    pallas_call x1, Pallas kernels, shards(): pl.pallas_call(sum_kernel, out_shape=(jax.ShapeDtypeStruct((class_local,...  17 us
    pallas_call x1, Pallas kernels, shards(): pl.pallas_call(score_kernel, out_shape=jax.ShapeDtypeStruct((half, LANES)...  14.5 us
    pallas_call x1, Pallas kernels, shards(): pl.pallas_call(reference_kernel, out_shape=(jax.ShapeDtypeStruct((class_l...  8.14 us
    pallas_call x1, Pallas kernels, shards(): pl.pallas_call(particle_kernel, out_shape=jax.ShapeDtypeStruct((home_coun...  6.13 us
  transfers between devices with their start and end apart: 2, of which 2 were waited for; matrix products, arithmetic and copies ran while one was open for 2% of the time, Pallas kernels for 3%

profile of v1, /device:TPU:0, one launch (start us, length us, event | category | flops | bytes accessed | tf_op | source)
XLA Modules:
  0.0 258.9 jit_solution(6876538995840747270)
XLA Ops:
  7.2 0.0 copy-start
  7.2 0.0 all-gather.3.cloned.1.call-start
  7.2 6.1 %align_particles.1 = bf16[48,48,128]{2,1,0:T(8,128)(2,1)} custom-call(s32[1]{0:T(128)} %bitcast.3.rot_ref, s32[48]{0:T(128)} %offset_ref.1, bf16[48,64,384]{2,1,0:T(8,128)(2,1)} %image_ref.2), custom_call_target="tpu_custom_call" | custom-call | tf_op jit(solution)/shard_map/align_particles/pallas_call | solution.py:199
  13.4 0.0 all-gather.3.cloned.1.call-update
  13.4 0.0 all-reduce.2.cloned.1.call-start
  13.4 28.2 %all-gather = s32[8,48,3]{1,2,0:T(4,128)S(1)} all-gather(s32[1,48,3]{1,2,0:T(4,128)} %bitcast.10), channel_id=1, replica_groups=mesh['cls'=8,'rot'=4] {'cls'}, dimensions={0}, use_global_device_ids=true | all-gather | bytes 5184 | tf_op jit(solution)/shard_map/all_gather | solution.py:178
  41.6 0.1 reshape.99
  41.7 0.6 convert_reduce_fusion
  43.0 0.0 copy-done
  43.0 0.1 dynamic-slice_bitcast_fusion
  43.1 0.7 copy.13.weight_ref
  43.8 0.2 select_reduce_fusion.3
  44.1 3.0 %select_reduce_fusion.2 = (s32[1160]{0:T(1024)S(1)}, s32[1160]{0:T(1024)S(1)}, s32[1160]{0:T(1024)S(1)}) fusion(s32[1152]{0:T(1024)S(1)} %select_reduce_fusion.3, pred[1152]{0:T(1024)(128)(4,1)S(1)} %fusion.3, s32[1152]{0:T(1024)S(1)} %get-tuple-element.13, s32[1152]{0:T(1024)S(1)} %get-tuple-element.14), kind=kLoop, calls=%fused_computation.2 | loop fusion | flops 10687080 | bytes 28896 | tf_op jit(solution)/shard_map/reduce_sum | solution.py:187
  47.1 8.1 %weight_references.1 = (bf16[64,128,128]{2,1,0:T(8,128)(2,1)}, f32[64,128]{1,0:T(8,128)}) custom-call(s32[1]{0:T(128)} %bitcast.3.rot_ref, bf16[64,64,384]{2,1,0:T(8,128)(2,1)} %image_ref.3, f32[16,1]{1,0:T(8,128)} %copy.13.weight_ref), custom_call_target="tpu_custom_call" | custom-call | tf_op jit(solution)/shard_map/weight_references/pallas_call | solution.py:217
  55.2 0.7 fusion.12
  55.9 0.6 pad_add_fusion.list_ref
  56.5 39.8 %all-gather.3.cloned.1.call-done.image_ref = bf16[384,48,128]{2,1,0:T(8,128)(2,1)} async-done(((bf16[48,48,128]{2,1,0:T(8,128)(2,1)}), bf16[384,48,128]{2,1,0:T(8,128)(2,1)}) %all-gather.3.cloned.1.call-update) | async-done | bytes 4718608 | tf_op jit(solution)/shard_map/all_gather | solution.py:214
  96.2 14.5 %score_pairs.1 = f32[576,128]{1,0:T(8,128)} custom-call(s32[1]{0:T(128)} %bitcast.2.count_ref, s32[3,1160]{1,0:T(4,128)} %pad_add_fusion.list_ref, bf16[384,48,128]{2,1,0:T(8,128)(2,1)} %all-gather.3.cloned.1.call-done.image_ref, bf16[64,128,128]{2,1,0:T(8,128)(2,1)} %get-tuple-element.6.class_ref, f32[64,128]{1,0:T(8,128)} %get-tuple-element.7.energy_ref), custom_call_target="tpu_custom_call" | custom-call | tf_op jit(solution)/shard_map/score_pairs/pallas_call | solution.py:239
  110.7 0.0 all-reduce.2.cloned.1.call-update
  110.8 122.9 %all-reduce.2.cloned.1.call-done.score_ref = f32[576,128]{1,0:T(8,128)} async-done(((f32[576,128]{1,0:T(8,128)}), f32[576,128]{1,0:T(8,128)}) %all-reduce.2.cloned.1.call-update) | async-done | bytes 294928 | tf_op jit(solution)/shard_map/psum | solution.py:248
  233.7 17.0 %sum_classes.1 = (f32[64,16,384]{2,1,0:T(8,128)}, f32[384,128]{1,0:T(8,128)}) custom-call(s32[1]{0:T(128)} %bitcast.2.count_ref, s32[3,1160]{1,0:T(4,128)} %pad_add_fusion.list_ref, f32[576,128]{1,0:T(8,128)} %all-reduce.2.cloned.1.call-done.score_ref, bf16[384,48,128]{2,1,0:T(8,128)(2,1)} %all-gather.3.cloned.1.call-done.image_ref), custom_call_target="tpu_custom_call" | custom-call | tf_op jit(solution)/shard_map/sum_classes/pallas_call | solution.py:250
  250.6 1.4 fusion.2
  (6 shorter events, 0.0 us)
Async XLA Ops:
  7.2 35.8 %copy-start = (f32[64]{0:T(128)S(1)}, f32[64]{0:T(128)}, u32[]{:S(2)}) copy-start(f32[64]{0:T(128)} %param.7) | copy-start | bytes 772
  7.2 89.1 %all-gather.3.cloned.1.call-start = ((), (), s32[]{:S(2)}) async-start(), calls=%async_computation | async-start | bytes 5308416 | tf_op jit(solution)/shard_map/all_gather | solution.py:214
  13.4 220.3 %all-reduce.2.cloned.1.call-start = ((), (), s32[]{:S(2)}) async-start(), calls=%async_computation.1 | async-start | bytes 589824 | tf_op jit(solution)/shard_map/psum | solution.py:248
Sparse Core Ops, SparseCore 0:
  13.5 82.6 all-gather.2
  110.9 122.7 all-reduce.1

commit v2 on v1

--- a/solution.py
+++ b/solution.py
@@ -12,6 +12,7 @@
 LANES = 128
 SPAN = LANES // GROUP
 BATCH = 8
+UNLISTED = -1e30
 F32 = jnp.float32
 BF16 = jnp.bfloat16
 
@@ -74,7 +75,7 @@
 
 
 def score_kernel(count_ref, list_ref, image_ref, class_ref, energy_ref, out_ref, held):
-    held[...] = jnp.zeros_like(held)
+    held[...] = jnp.full_like(held, UNLISTED)
     half = out_ref.shape[0]
 
     def batch(step, carry):
@@ -97,29 +98,111 @@
     low = pltpu.roll(held[pl.ds(0, half), :], LANES - ROTS, 1)
     high = pltpu.roll(held[pl.ds(half, half), :], LANES // 2 - ROTS, 1)
     inside = (lane % (LANES // 2)) < ROTS
-    out_ref[...] = jnp.where(inside, jnp.where(lane < LANES // 2, low, high), 0.0)
+    out_ref[...] = jnp.where(inside, jnp.where(lane < LANES // 2, low, high), UNLISTED)
+
+
+def push(peers, source, inbox, sends, arrivals):
+    copies = [
+        pltpu.make_async_remote_copy(
+            src_ref=source(peer),
+            dst_ref=inbox.at[slot],
+            send_sem=sends.at[slot],
+            recv_sem=arrivals.at[slot],
+            device_id=peer,
+            device_id_type=pl.DeviceIdType.MESH,
+        )
+        for slot, peer in enumerate(peers)
+    ]
+    for copy in copies:
+        copy.start()
+    return copies
+
+
+def peers_along(axis):
+    size = lax.axis_size(axis)
+    own = lax.axis_index(axis)
+    return [{axis: lax.rem(own + step, size)} for step in range(1, size)]
+
+
+def greet(peers):
+    barrier = pltpu.get_barrier_semaphore()
+    for peer in peers:
+        pl.semaphore_signal(barrier, inc=1, device_id=peer, device_id_type=pl.DeviceIdType.MESH)
+    pl.semaphore_wait(barrier, len(peers))
+
+
+def list_kernel(own_ref, out_ref, inbox, sends, arrivals):
+    peers = peers_along("cls")
+    size = len(peers) + 1
+    me = lax.axis_index("cls")
+    greet(peers)
+    copies = push(peers, lambda peer: own_ref, inbox, sends, arrivals)
+    out_ref[me] = own_ref[...]
+    for slot, copy in enumerate(copies):
+        copy.wait_recv()
+        out_ref[lax.rem(me + size - slot - 1, size)] = inbox[slot]
+    for copy in copies:
+        copy.wait_send()
+
+
+def reduce_kernel(
+    score_ref, out_ref, pair_ref, parts, share, spread, tally, tallies, summed, wide,
+    send_a, send_b, send_c, send_d, recv_a, recv_b, recv_c, recv_d,
+):
+    rots, owners = peers_along("rot"), peers_along("cls")
+    splits = len(rots) + 1
+    rot = lax.axis_index("rot")
+    rows = share.shape[0]
+    greet(rots + owners)
+
+    def part(index):
+        return pl.ds(pl.multiple_of(index * rows, GROUP), rows)
+
+    first = push(rots, lambda peer: score_ref.at[part(peer["rot"])], parts, send_a, recv_a)
+    total = score_ref[part(rot), :]
+    for slot, copy in enumerate(first):
+        copy.wait_recv()
+        total = total + parts[slot]
+    share[...] = total
+    second = push(rots, lambda peer: share, spread, send_b, recv_b)
+    grown = jnp.concatenate(
+        [jnp.exp(total), jnp.zeros((tally.shape[1] - rows, LANES), F32)], axis=0
+    ).T
+    tally[...] = jnp.zeros_like(tally)
+    tally[pl.ds(0, 1), :] = jnp.sum(grown[: LANES // 2], axis=0, keepdims=True)
+    tally[pl.ds(1, 1), :] = jnp.sum(grown[LANES // 2 :], axis=0, keepdims=True)
+    third = push(owners, lambda peer: tally, tallies, send_c, recv_c)
+    out_ref[part(rot), :] = total
+    sums = tally[...]
+    for slot, copy in enumerate(third):
+        copy.wait_recv()
+        sums = sums + tallies[slot]
+    summed[...] = sums
+    fourth = push(rots, lambda peer: summed, wide, send_d, recv_d)
+    pair_ref[rot] = sums
+    for slot in range(len(rots)):
+        source = lax.rem(rot + splits - slot - 1, splits)
+        second[slot].wait_recv()
+        out_ref[part(source), :] = spread[slot]
+        fourth[slot].wait_recv()
+        pair_ref[source] = wide[slot]
+    for copy in first + second + third + fourth:
+        copy.wait_send()
 
 
 def sum_kernel(
-    count_ref, list_ref, score_ref, image_ref, out_ref, total_ref, weight, sums, flipped
+    count_ref, list_ref, score_ref, total_ref, image_ref, out_ref, weight, sums, flipped
 ):
     half = score_ref.shape[0]
     particles = total_ref.shape[0]
     class_local, cycles, angles = out_ref.shape
     lane = lax.broadcasted_iota(jnp.int32, (half, LANES), 1)
-    inside = (lane % (LANES // 2)) < ROTS
-    grown = jnp.where(inside, jnp.exp(score_ref[...]), 0.0)
+    grown = jnp.exp(score_ref[...])
     lows = jnp.where(lane < LANES // 2, grown, 0.0)
-    highs = pltpu.roll(grown - lows, LANES // 2, 1)
     weight[pl.ds(0, half), :] = lows
-    weight[pl.ds(half, half), :] = highs
-    listed = 2 * half // particles
-    total = jnp.zeros((particles, 1), F32)
-    for k in range(listed):
-        total += jnp.sum(weight[pl.ds(k * particles, particles), :], axis=1, keepdims=True)
-    total_ref[...] = jnp.broadcast_to(total, total_ref.shape)
-    inverse = 1.0 / total
-    for k in range(listed):
+    weight[pl.ds(half, half), :] = pltpu.roll(grown - lows, LANES // 2, 1)
+    inverse = 1.0 / total_ref[...]
+    for k in range(2 * half // particles):
         rows = pl.ds(k * particles, particles)
         posterior = weight[rows, :] * inverse
         weight[rows, :] = posterior + pltpu.roll(posterior, LANES - ROTS, 1)
@@ -175,8 +258,21 @@
     rot_arg = rot.reshape(1)
     limit = pltpu.CompilerParams(vmem_limit_bytes=56 << 20)
 
-    classes = lax.all_gather(sig_classes, "cls", axis=0, tiled=True)
-    classes = classes.T.reshape(pair_count)
+    owners, rots = owner_count - 1, split_count - 1
+    own_list = jnp.pad(
+        sig_classes.T, ((0, GROUP - list_length), (0, LANES - home_count)), constant_values=0
+    )
+    classes = pl.pallas_call(
+        list_kernel,
+        out_shape=jax.ShapeDtypeStruct((owner_count, GROUP, LANES), jnp.int32),
+        in_specs=[VMEM],
+        out_specs=VMEM,
+        scratch_shapes=[pltpu.VMEM((owners, GROUP, LANES), jnp.int32)]
+        + [pltpu.SemaphoreType.DMA((owners,))] * 2,
+        compiler_params=pltpu.CompilerParams(collective_id=1, has_side_effects=True),
+        name="exchange_lists",
+    )(own_list)
+    classes = classes[:, :list_length, :home_count].transpose(1, 0, 2).reshape(pair_count)
     pair_iota = jnp.arange(pair_count, dtype=jnp.int32)
     mine = (classes // class_local) == me
     before = pair_iota[None, :] < pair_iota[:, None]
@@ -245,16 +341,40 @@
         compiler_params=limit,
         name="score_pairs",
     )(batches, work, gathered, class_pages, energy)
-    scores = lax.psum(scores, ("cls", "rot"))
-
-    class_sums, total = pl.pallas_call(
+    share = half // split_count
+    wide = -(-share // LANES) * LANES
+    tile = pltpu.VMEM((GROUP, wide), F32)
+    scores, pair_sums = pl.pallas_call(
+        reduce_kernel,
+        out_shape=(
+            jax.ShapeDtypeStruct((half, LANES), F32),
+            jax.ShapeDtypeStruct((split_count, GROUP, wide), F32),
+        ),
+        in_specs=[VMEM],
+        out_specs=(VMEM, VMEM),
+        scratch_shapes=[
+            pltpu.VMEM((rots, share, LANES), F32),
+            pltpu.VMEM((share, LANES), F32),
+            pltpu.VMEM((rots, share, LANES), F32),
+            tile,
+            pltpu.VMEM((owners, GROUP, wide), F32),
+            tile,
+            pltpu.VMEM((rots, GROUP, wide), F32),
+        ]
+        + [pltpu.SemaphoreType.DMA((count_of,)) for count_of in (rots, rots, owners, rots)] * 2,
+        compiler_params=pltpu.CompilerParams(
+            collective_id=2, has_side_effects=True, vmem_limit_bytes=56 << 20
+        ),
+        name="exchange_scores",
+    )(scores)
+    pair_sums = pair_sums[:, :2, :share].transpose(1, 0, 2).reshape(list_length, particle_count)
+    total = jnp.sum(pair_sums, axis=0)
+
+    class_sums = pl.pallas_call(
         sum_kernel,
-        out_shape=(
-            jax.ShapeDtypeStruct((class_local, cycles, angle_count), F32),
-            jax.ShapeDtypeStruct((particle_count, LANES), F32),
-        ),
-        in_specs=[SMEM, SMEM, VMEM, VMEM],
-        out_specs=(VMEM, VMEM),
+        out_shape=jax.ShapeDtypeStruct((class_local, cycles, angle_count), F32),
+        in_specs=[SMEM, SMEM, VMEM, VMEM, VMEM],
+        out_specs=VMEM,
         scratch_shapes=[
             pltpu.VMEM((pair_count + GROUP, LANES), F32),
             pltpu.VMEM((class_local, ROTS, LANES), F32),
@@ -262,8 +382,8 @@
         ],
         compiler_params=limit,
         name="sum_classes",
-    )(batches, work, scores, gathered)
-    own_total = lax.dynamic_slice_in_dim(total, me * home_count, home_count)[:, 0]
+    )(batches, work, scores, total.reshape(particle_count, 1), gathered)
+    own_total = lax.dynamic_slice_in_dim(total, me * home_count, home_count)
     return (jnp.log(own_total), class_sums)
 
 

time: 260 us -> 150 us (0.58)
  waiting for transfers between devices: 163 us -> 55.4 us
  blocking collectives: 28.2 us -> 0 us
  Pallas kernels: 45.7 us -> 70 us
  local copies, waits for them, and re-layouts: 2.23 us -> 5.14 us
    psum x1 -> x0, waiting for transfers between devices: 123 us -> none  [shards(): scores = lax.psum(scores, ('cls', 'rot'))]
    all_gather x1 -> x0, blocking collectives: 28.2 us -> none  [shards(): classes = lax.all_gather(sig_classes, 'cls', axis=0, tiled=True)]
    pallas_call x1 -> x3, Pallas kernels: 17 us -> 41.2 us  [the longest x1 17 us: shards(): pl.pallas_call(sum_kernel, out_shape=jax.ShapeDtypeStruct((class_local, c...]
    all_gather x1, waiting for transfers between devices: 39.8 us -> 55.3 us  [shards(): gathered = lax.all_gather(pages, 'cls', axis=0, tiled=True)]
  transfers between devices with their start and end apart: 2 -> 1, of which waited for: 2 -> 1; matrix products, arithmetic and copies ran while one was open for 2% -> 6% of each run, Pallas kernels for 3% -> 12%
where the time goes in v2:
time: 150 us; the launch traced here: 151 us
  Pallas kernels  70 us (47%)
  waiting for transfers between devices  55.4 us (37%)
  between operations  14.8 us (10%)
  other arithmetic  5.96 us (4%)
  local copies, waits for them, and re-layouts  5.14 us (3%)
    all_gather x1, waiting for transfers between devices, shards(): gathered = lax.all_gather(pages, 'cls', axis=0, tiled=True)  55.3 us
    pallas_call x1, Pallas kernels, shards(): pl.pallas_call(sum_kernel, out_shape=jax.ShapeDtypeStruct((class_local, c...  17 us
    pallas_call x1, Pallas kernels, shards(): pl.pallas_call(reduce_kernel, out_shape=(jax.ShapeDtypeStruct((half, LANE...  14.6 us
    pallas_call x1, Pallas kernels, shards(): pl.pallas_call(score_kernel, out_shape=jax.ShapeDtypeStruct((half, LANES)...  14.5 us
    pallas_call x1, Pallas kernels, shards(): pl.pallas_call(list_kernel, out_shape=jax.ShapeDtypeStruct((owner_count,...  9.71 us
    pallas_call x1, Pallas kernels, shards(): pl.pallas_call(reference_kernel, out_shape=(jax.ShapeDtypeStruct((class_l...  8.12 us
    pallas_call x1, Pallas kernels, shards(): pl.pallas_call(particle_kernel, out_shape=jax.ShapeDtypeStruct((home_coun...  6.13 us
  transfers between devices with their start and end apart: 1, of which 1 were waited for; matrix products, arithmetic and copies ran while one was open for 6% of the time, Pallas kernels for 12%

profile of v2, /device:TPU:0, one launch (start us, length us, event | category | flops | bytes accessed | tf_op | source)
XLA Modules:
  0.0 151.3 jit_solution(948513004750073845)
XLA Ops:
  7.2 0.0 copy-start
  7.2 0.0 all-gather.2.cloned.1.call-start
  7.2 6.1 %align_particles.1 = bf16[48,48,128]{2,1,0:T(8,128)(2,1)} custom-call(s32[1]{0:T(128)} %bitcast.3.rot_ref, s32[48]{0:T(128)} %offset_ref.1, bf16[48,64,384]{2,1,0:T(8,128)(2,1)} %image_ref.2), custom_call_target="tpu_custom_call" | custom-call | tf_op jit(solution)/shard_map/align_particles/pallas_call | solution.py:295
  13.4 0.0 all-gather.2.cloned.1.call-update
  13.4 1.3 pad.4.own_ref
  14.7 9.7 %exchange_lists.1 = s32[8,8,128]{2,1,0:T(8,128)} custom-call(s32[8,128]{1,0:T(8,128)} %pad.4.own_ref), custom_call_target="tpu_custom_call" | custom-call | tf_op jit(solution)/shard_map/exchange_lists/pallas_call | solution.py:265
  24.4 1.4 convert_reduce_fusion
  26.5 0.0 copy-done
  26.5 0.1 dynamic-slice_bitcast_fusion
  26.6 0.7 copy.17.weight_ref
  27.2 0.8 slice_bitcast_fusion
  28.0 0.1 reshape.100
  28.1 0.2 select_reduce_fusion.3
  28.4 3.0 %select_reduce_fusion.2 = (s32[1160]{0:T(1024)S(1)}, s32[1160]{0:T(1024)S(1)}, s32[1160]{0:T(1024)S(1)}) fusion(s32[1152]{0:T(1024)S(1)} %select_reduce_fusion.3, pred[1152]{0:T(1024)(128)(4,1)S(1)} %fusion.5, s32[1152]{0:T(1024)S(1)} %get-tuple-element.13, s32[1152]{0:T(1024)S(1)} %get-tuple-element.14), kind=kLoop, calls=%fused_computation.2 | loop fusion | flops 10687080 | bytes 28896 | tf_op jit(solution)/shard_map/reduce_sum | solution.py:283
  31.4 8.1 %weight_references.1 = (bf16[64,128,128]{2,1,0:T(8,128)(2,1)}, f32[64,128]{1,0:T(8,128)}) custom-call(s32[1]{0:T(128)} %bitcast.3.rot_ref, bf16[64,64,384]{2,1,0:T(8,128)(2,1)} %image_ref.3, f32[16,1]{1,0:T(8,128)} %copy.17.weight_ref), custom_call_target="tpu_custom_call" | custom-call | tf_op jit(solution)/shard_map/weight_references/pallas_call | solution.py:313
  39.5 0.7 fusion.11
  40.2 0.6 pad_add_fusion.list_ref
  40.8 55.3 %all-gather.2.cloned.1.call-done.image_ref = bf16[384,48,128]{2,1,0:T(8,128)(2,1)} async-done(((bf16[48,48,128]{2,1,0:T(8,128)(2,1)}), bf16[384,48,128]{2,1,0:T(8,128)(2,1)}) %all-gather.2.cloned.1.call-update) | async-done | bytes 4718608 | tf_op jit(solution)/shard_map/all_gather | solution.py:310
  96.1 14.5 %score_pairs.1.score_ref = f32[576,128]{1,0:T(8,128)} custom-call(s32[1]{0:T(128)} %bitcast.2.count_ref, s32[3,1160]{1,0:T(4,128)} %pad_add_fusion.list_ref, bf16[384,48,128]{2,1,0:T(8,128)(2,1)} %all-gather.2.cloned.1.call-done.image_ref, bf16[64,128,128]{2,1,0:T(8,128)(2,1)} %get-tuple-element.6.class_ref, f32[64,128]{1,0:T(8,128)} %get-tuple-element.7.energy_ref), custom_call_target="tpu_custom_call" | custom-call | tf_op jit(solution)/shard_map/score_pairs/pallas_call | solution.py:335
  110.6 14.6 %exchange_scores.1 = (f32[576,128]{1,0:T(8,128)}, f32[4,8,256]{2,1,0:T(8,128)}) custom-call(f32[576,128]{1,0:T(8,128)} %score_pairs.1.score_ref), custom_call_target="tpu_custom_call" | custom-call | tf_op jit(solution)/shard_map/exchange_scores/pallas_call | solution.py:347
  125.2 0.8 slice_bitcast_fusion.1
  126.0 0.1 reshape.103
  126.1 0.8 reshape.105.total_ref
  126.9 0.6 dynamic-slice_log_fusion
  127.5 17.0 %sum_classes.1 = f32[64,16,384]{2,1,0:T(8,128)} custom-call(s32[1]{0:T(128)} %bitcast.2.count_ref, s32[3,1160]{1,0:T(4,128)} %pad_add_fusion.list_ref, f32[576,128]{1,0:T(8,128)} %get-tuple-element.9.score_ref, f32[384,1]{1,0:T(8,128)} %reshape.105.total_ref, bf16[384,48,128]{2,1,0:T(8,128)(2,1)} %all-gather.2.cloned.1.call-done.image_ref), custom_call_target="tpu_custom_call" | custom-call | tf_op jit(solution)/shard_map/sum_classes/pallas_call | solution.py:373
  (7 shorter events, 0.1 us)
Async XLA Ops:
  7.2 19.3 %copy-start = (f32[64]{0:T(128)S(1)}, f32[64]{0:T(128)}, u32[]{:S(2)}) copy-start(f32[64]{0:T(128)} %param.7) | copy-start | bytes 772
  7.2 88.9 %all-gather.2.cloned.1.call-start = ((), (), s32[]{:S(2)}) async-start(), calls=%async_computation | async-start | bytes 5308416 | tf_op jit(solution)/shard_map/all_gather | solution.py:310
Sparse Core Ops, SparseCore 0:
  13.5 82.5 all-gather.1

commit v3 on v2

--- a/solution.py
+++ b/solution.py
@@ -131,18 +131,58 @@
     pl.semaphore_wait(barrier, len(peers))
 
 
-def list_kernel(own_ref, out_ref, inbox, sends, arrivals):
+def gather_kernel(
+    page_ref, own_ref, out_ref, list_ref, inbox, local_sem, list_sends, list_arrivals, sends, arrivals
+):
     peers = peers_along("cls")
     size = len(peers) + 1
     me = lax.axis_index("cls")
+    steps = size // 2
+    part = page_ref.shape[0] // 2
+    odd = lax.rem(me, 2)
+    spot = odd * (size - 1 - me // 2) + (1 - odd) * (me // 2)
+
+    def index_at(position):
+        position = lax.rem(position + size, size)
+        back = position // steps
+        return (1 - back) * 2 * position + back * (2 * (size - 1 - position) + 1)
+
+    nexts = (index_at(spot + 1), index_at(spot - 1))
     greet(peers)
-    copies = push(peers, lambda peer: own_ref, inbox, sends, arrivals)
-    out_ref[me] = own_ref[...]
-    for slot, copy in enumerate(copies):
+    lists = push(peers, lambda peer: own_ref, inbox, list_sends, list_arrivals)
+    local = pltpu.make_async_copy(page_ref, out_ref.at[me], local_sem)
+    local.start()
+    copies, pending = {}, []
+    for step in range(steps):
+        for piece in (0, 1):
+            for way in (0, 1):
+                if step == steps - 1 and way != piece:
+                    continue
+                rows = pl.ds(piece * part, part)
+                owner = index_at(spot - step if way == 0 else spot + step)
+                if step:
+                    copies[way, step - 1, piece].wait_recv()
+                    pending.remove((way, step - 1, piece))
+                copy = pltpu.make_async_remote_copy(
+                    src_ref=out_ref.at[owner, rows] if step else page_ref.at[rows],
+                    dst_ref=out_ref.at[owner, rows],
+                    send_sem=sends.at[way, step, piece],
+                    recv_sem=arrivals.at[way, step, piece],
+                    device_id={"cls": nexts[way]},
+                    device_id_type=pl.DeviceIdType.MESH,
+                )
+                copy.start()
+                copies[way, step, piece] = copy
+                pending.append((way, step, piece))
+    list_ref[me] = own_ref[...]
+    for slot, copy in enumerate(lists):
         copy.wait_recv()
-        out_ref[lax.rem(me + size - slot - 1, size)] = inbox[slot]
-    for copy in copies:
+        list_ref[lax.rem(me + size - slot - 1, size)] = inbox[slot]
+    for key in pending:
+        copies[key].wait_recv()
+    for copy in lists + list(copies.values()):
         copy.wait_send()
+    local.wait()
 
 
 def reduce_kernel(
@@ -262,16 +302,45 @@
     own_list = jnp.pad(
         sig_classes.T, ((0, GROUP - list_length), (0, LANES - home_count)), constant_values=0
     )
-    classes = pl.pallas_call(
-        list_kernel,
-        out_shape=jax.ShapeDtypeStruct((owner_count, GROUP, LANES), jnp.int32),
-        in_specs=[VMEM],
-        out_specs=VMEM,
-        scratch_shapes=[pltpu.VMEM((owners, GROUP, LANES), jnp.int32)]
-        + [pltpu.SemaphoreType.DMA((owners,))] * 2,
-        compiler_params=pltpu.CompilerParams(collective_id=1, has_side_effects=True),
-        name="exchange_lists",
-    )(own_list)
+    image_block = (GROUP, cycles, angle_count)
+    pages = pl.pallas_call(
+        particle_kernel,
+        out_shape=jax.ShapeDtypeStruct((home_count, ROTS, LANES), BF16),
+        grid_spec=pltpu.PrefetchScalarGridSpec(
+            num_scalar_prefetch=2,
+            grid=(home_count // GROUP,),
+            in_specs=[pl.BlockSpec(image_block, lambda g, r, o: (g, r[0], 0))],
+            out_specs=pl.BlockSpec((GROUP, ROTS, LANES), lambda g, r, o: (g, 0, 0)),
+            scratch_shapes=[
+                pltpu.VMEM((LANES, angle_count), F32),
+                pltpu.VMEM((angle_count, LANES), F32),
+            ],
+        ),
+        name="align_particles",
+    )(rot_arg, offsets, particles)
+    ring = pltpu.SemaphoreType.DMA((2, owner_count // 2, 2))
+    gathered, classes = pl.pallas_call(
+        gather_kernel,
+        out_shape=(
+            jax.ShapeDtypeStruct((owner_count,) + pages.shape, BF16),
+            jax.ShapeDtypeStruct((owner_count, GROUP, LANES), jnp.int32),
+        ),
+        in_specs=[VMEM, VMEM],
+        out_specs=(pl.BlockSpec(memory_space=pl.ANY), VMEM),
+        scratch_shapes=[
+            pltpu.VMEM((owners, GROUP, LANES), jnp.int32),
+            pltpu.SemaphoreType.DMA,
+            pltpu.SemaphoreType.DMA((owners,)),
+            pltpu.SemaphoreType.DMA((owners,)),
+            ring,
+            ring,
+        ],
+        compiler_params=pltpu.CompilerParams(
+            collective_id=1, has_side_effects=True, vmem_limit_bytes=56 << 20
+        ),
+        name="gather_particles",
+    )(pages, own_list)
+    gathered = gathered.reshape(particle_count, ROTS, LANES)
     classes = classes[:, :list_length, :home_count].transpose(1, 0, 2).reshape(pair_count)
     pair_iota = jnp.arange(pair_count, dtype=jnp.int32)
     mine = (classes // class_local) == me
@@ -291,24 +360,6 @@
     )
     batches = ((count + BATCH - 1) // BATCH).reshape(1)
 
-    image_block = (GROUP, cycles, angle_count)
-    pages = pl.pallas_call(
-        particle_kernel,
-        out_shape=jax.ShapeDtypeStruct((home_count, ROTS, LANES), BF16),
-        grid_spec=pltpu.PrefetchScalarGridSpec(
-            num_scalar_prefetch=2,
-            grid=(home_count // GROUP,),
-            in_specs=[pl.BlockSpec(image_block, lambda g, r, o: (g, r[0], 0))],
-            out_specs=pl.BlockSpec((GROUP, ROTS, LANES), lambda g, r, o: (g, 0, 0)),
-            scratch_shapes=[
-                pltpu.VMEM((LANES, angle_count), F32),
-                pltpu.VMEM((angle_count, LANES), F32),
-            ],
-        ),
-        name="align_particles",
-    )(rot_arg, offsets, particles)
-    gathered = lax.all_gather(pages, "cls", axis=0, tiled=True)
-
     own_weights = lax.dynamic_slice_in_dim(noise_weights, rot * cycles, cycles).reshape(cycles, 1)
     class_pages, energy = pl.pallas_call(
         reference_kernel,

time: 150 us -> 127 us (0.85)
  waiting for transfers between devices: 55.4 us -> 0 us
  Pallas kernels: 70 us -> 115 us
  between operations: 14.8 us -> 1.39 us
    all_gather x1 -> x0, waiting for transfers between devices: 55.3 us -> none  [shards(): gathered = lax.all_gather(pages, 'cls', axis=0, tiled=True)]
    pallas_call x1, Pallas kernels: 9.71 us -> 55 us  [shards(): pl.pallas_call(gather_kernel, out_shape=(jax.ShapeDtypeStruct((owner_coun...]
  transfers between devices with their start and end apart: 1 -> 0, of which waited for: 1 -> 0; matrix products, arithmetic and copies ran while one was open for 6% -> 0% of each run, Pallas kernels for 12% -> 0%
where the time goes in v3:
time: 127 us; the launch traced here: 128 us
  Pallas kernels  115 us (91%)
  other arithmetic  5.97 us (5%)
  local copies, waits for them, and re-layouts  5.15 us (4%)
  between operations  1.39 us (1%)
    pallas_call x1, Pallas kernels, shards(): pl.pallas_call(gather_kernel, out_shape=(jax.ShapeDtypeStruct((owner_coun...  55 us
    pallas_call x1, Pallas kernels, shards(): pl.pallas_call(sum_kernel, out_shape=jax.ShapeDtypeStruct((class_local, c...  17 us
    pallas_call x1, Pallas kernels, shards(): pl.pallas_call(reduce_kernel, out_shape=(jax.ShapeDtypeStruct((half, LANE...  14.6 us
    pallas_call x1, Pallas kernels, shards(): pl.pallas_call(score_kernel, out_shape=jax.ShapeDtypeStruct((half, LANES)...  14.5 us
    pallas_call x1, Pallas kernels, shards(): pl.pallas_call(reference_kernel, out_shape=(jax.ShapeDtypeStruct((class_l...  8.1 us
    pallas_call x1, Pallas kernels, shards(): pl.pallas_call(particle_kernel, out_shape=jax.ShapeDtypeStruct((home_coun...  6.13 us
    reduce_sum x1, other arithmetic, shards(): pick = lambda values: jnp.sum(jnp.where(hit, values[None, :], 0), axis=1)  2.98 us

profile of v3, /device:TPU:0, one launch (start us, length us, event | category | flops | bytes accessed | tf_op | source)
XLA Modules:
  0.0 127.7 jit_solution(1063814855126411857)
XLA Ops:
  0.6 0.0 copy-start
  0.7 6.1 %align_particles.1.page_ref = bf16[48,48,128]{2,1,0:T(8,128)(2,1)} custom-call(s32[1]{0:T(128)} %bitcast.rot_ref, s32[48]{0:T(128)} %offset_ref.1, bf16[48,64,384]{2,1,0:T(8,128)(2,1)} %image_ref.2), custom_call_target="tpu_custom_call" | custom-call | tf_op jit(solution)/shard_map/align_particles/pallas_call | solution.py:306
  6.8 1.3 pad.4.own_ref
  8.1 55.0 %gather_particles.1 = (bf16[8,48,48,128]{3,2,1,0:T(8,128)(2,1)}, s32[8,8,128]{2,1,0:T(8,128)}) custom-call(bf16[48,48,128]{2,1,0:T(8,128)(2,1)} %align_particles.1.page_ref, s32[8,128]{1,0:T(8,128)} %pad.4.own_ref), custom_call_target="tpu_custom_call" | custom-call | tf_op jit(solution)/shard_map/gather_particles/pallas_call | solution.py:322
  63.0 0.8 slice_bitcast_fusion
  63.8 0.1 reshape.104
  63.9 0.3 select_reduce_fusion.3
  64.2 3.0 %select_reduce_fusion.2 = (s32[1160]{0:T(1024)S(1)}, s32[1160]{0:T(1024)S(1)}, s32[1160]{0:T(1024)S(1)}) fusion(s32[1152]{0:T(1024)S(1)} %select_reduce_fusion.3, pred[1152]{0:T(1024)(128)(4,1)S(1)} %fusion.5, s32[1152]{0:T(1024)S(1)} %get-tuple-element.17, s32[1152]{0:T(1024)S(1)} %get-tuple-element.18), kind=kLoop, calls=%fused_computation.2 | loop fusion | flops 10687080 | bytes 28896 | tf_op jit(solution)/shard_map/reduce_sum | solution.py:352
  67.1 1.4 %convert_reduce_fusion = s32[]{:T(128)} fusion(s32[]{:T(128)S(6)} %axis_index.25, s32[8,8,128]{2,1,0:T(8,128)} %get-tuple-element.8), kind=kLoop, calls=%fused_computation.16 | loop fusion | flops 20735 | bytes 4616 | tf_op jit(solution)/shard_map/reduce_sum | solution.py:349
  68.6 0.7 fusion.11
  69.2 0.6 pad_add_fusion.list_ref
  70.5 0.0 copy-done
  70.6 0.1 dynamic-slice_bitcast_fusion
  70.6 0.7 copy.13.weight_ref
  71.3 8.1 %weight_references.1 = (bf16[64,128,128]{2,1,0:T(8,128)(2,1)}, f32[64,128]{1,0:T(8,128)}) custom-call(s32[1]{0:T(128)} %bitcast.rot_ref, bf16[64,64,384]{2,1,0:T(8,128)(2,1)} %image_ref.3, f32[16,1]{1,0:T(8,128)} %copy.13.weight_ref), custom_call_target="tpu_custom_call" | custom-call | tf_op jit(solution)/shard_map/weight_references/pallas_call | solution.py:364
  79.4 14.5 %score_pairs.1.score_ref = f32[576,128]{1,0:T(8,128)} custom-call(s32[1]{0:T(128)} %bitcast.3.count_ref, s32[3,1160]{1,0:T(4,128)} %pad_add_fusion.list_ref, bf16[384,48,128]{2,1,0:T(8,128)(2,1)} %bitcast.12, bf16[64,128,128]{2,1,0:T(8,128)(2,1)} %get-tuple-element.10.class_ref, f32[64,128]{1,0:T(8,128)} %get-tuple-element.11.energy_ref), custom_call_target="tpu_custom_call" | custom-call | tf_op jit(solution)/shard_map/score_pairs/pallas_call | solution.py:386
  93.9 14.6 %exchange_scores.1 = (f32[576,128]{1,0:T(8,128)}, f32[4,8,256]{2,1,0:T(8,128)}) custom-call(f32[576,128]{1,0:T(8,128)} %score_pairs.1.score_ref), custom_call_target="tpu_custom_call" | custom-call | tf_op jit(solution)/shard_map/exchange_scores/pallas_call | solution.py:398
  108.5 0.8 slice_bitcast_fusion.1
  109.3 0.1 reshape.107
  109.4 0.8 reshape.109.total_ref
  110.2 17.0 %sum_classes.1 = f32[64,16,384]{2,1,0:T(8,128)} custom-call(s32[1]{0:T(128)} %bitcast.3.count_ref, s32[3,1160]{1,0:T(4,128)} %pad_add_fusion.list_ref, f32[576,128]{1,0:T(8,128)} %get-tuple-element.13.score_ref, f32[384,1]{1,0:T(8,128)} %reshape.109.total_ref, bf16[384,48,128]{2,1,0:T(8,128)(2,1)} %bitcast.13), custom_call_target="tpu_custom_call" | custom-call | tf_op jit(solution)/shard_map/sum_classes/pallas_call | solution.py:424
  127.1 0.6 dynamic-slice_log_fusion
  (7 shorter events, 0.1 us)
Async XLA Ops:
  0.6 69.9 %copy-start = (f32[64]{0:T(128)S(1)}, f32[64]{0:T(128)}, u32[]{:S(2)}) copy-start(f32[64]{0:T(128)} %param.7) | copy-start | bytes 772
